TPU v7x, 256 devices: a whole 4x4x8 slice. The times are simulated.
256 devices in a mesh: expert: 64 (over y, z, core), tensor: 4 (over x).
Axes of the slice: x: 4, y: 4, z: 8, core: 2. Of those that a mesh axis runs over, the one named last changes fastest.
Arguments:
- activations: bfloat16 [32768, 4096], P(('expert', 'tensor')), may hold values from -6 to 6
- out_grad: bfloat16 [32768, 4096], P(('expert', 'tensor')), may hold values from -6 to 6
- expert_ids: int32 [32768, 1], P('expert'), may hold values from 0 to 63; in each aligned block of 128 rows (0 to 127, 128 to 255, ...) at most 3 rows name the same one
- gate_weights: bfloat16 [32768, 1], P('expert'), may hold values from 0.049804688 to 1
- weight_in: bfloat16 [64, 4096, 1536], P('expert', None, 'tensor'), may hold values from -0.09375 to 0.09375
- weight_out: bfloat16 [64, 1536, 4096], P('expert', 'tensor'), may hold values from -0.15625 to 0.15625
Outputs:
- grad_in: bfloat16 [32768, 4096], P(('expert', 'tensor'))
- grad_gates: float32 [32768, 1], P(('expert', 'tensor'))
- grad_weight_out: bfloat16 [64, 1536, 4096], P('expert', 'tensor')
Inputs may be any that keep to these rules, and one draw needn't show every extreme that they name: `expert_ids`: each token names 1 different experts. Among the 128 tokens of one device (aligned blocks of rows) no expert is named by more than 3 tokens, and in every draw some expert is named by exactly 3 tokens of some device.
All inputs are finite; a program needn't handle non-finite values.
Results may differ from a plain program's by a relative error of at most 0.013.
Values may be sent and summed in bfloat16 or wider, within the bound.
No kernel may reach another device: no remote copies, remote signals or barrier semaphores. Data moves between devices by JAX's collectives and lax.ppermute only.
A program may use at most 128 MiB of HBM per device.

v0:
```python
import jax
import jax.numpy as jnp
from jax import lax
from jax.sharding import PartitionSpec as P

EXPERTS = 64
CAP = 3


ROOT_HALF = 0.7071067811865476
INV_ROOT_TAU = 0.3989422804014327


def slot_places(expert_ids, num_blocks, capacity, num_experts):
    row_count = expert_ids.shape[0]
    block_rows = row_count // num_blocks
    matches = (expert_ids[:, :, None] == jnp.arange(num_experts, dtype=jnp.int32)).astype(jnp.int32)
    chosen = jnp.sum(matches, axis=1).reshape(num_blocks, block_rows, num_experts)
    earlier = (jnp.cumsum(chosen, axis=1) - chosen).reshape(row_count, num_experts)
    position = jnp.sum(matches * earlier[:, None, :], axis=2)
    block_index = (jnp.arange(row_count, dtype=jnp.int32) // block_rows)[:, None]
    return expert_ids * (num_blocks * capacity) + block_index * capacity + position


def pick_table(places, total_slots):
    return (places[:, :, None] == jnp.arange(total_slots, dtype=jnp.int32)).astype(jnp.float32)


def pack_slots(table, token_rows, grad_rows, gate_rows):
    spread = jnp.sum(table, axis=1).astype(jnp.bfloat16)
    packed_in = jnp.dot(spread.T, token_rows, preferred_element_type=jnp.float32).astype(
        jnp.bfloat16
    )
    packed_grad = jnp.dot(spread.T, grad_rows, preferred_element_type=jnp.float32).astype(
        jnp.bfloat16
    )
    packed_gate = jnp.sum(table * gate_rows.astype(jnp.float32)[:, :, None], axis=(0, 1)).astype(
        jnp.bfloat16
    )
    return (packed_in, packed_grad, packed_gate)


def expert_math(inputs, grad_rows, gate_rows, weight_in, weight_out):
    before_act = jnp.einsum("slcd,ldf->slcf", inputs, weight_in, preferred_element_type=jnp.float32)
    normal_cdf = 0.5 * (1.0 + lax.erf(before_act * ROOT_HALF))
    activated = (before_act * normal_cdf).astype(jnp.bfloat16)
    derivative = normal_cdf + before_act * INV_ROOT_TAU * jnp.exp(-0.5 * before_act * before_act)
    expert_out = jnp.einsum(
        "slcf,lfd->slcd", activated, weight_out, preferred_element_type=jnp.float32
    )
    scores = jnp.sum(expert_out * grad_rows.astype(jnp.float32), axis=-1)
    scaled = (gate_rows.astype(jnp.float32)[..., None] * grad_rows.astype(jnp.float32)).astype(
        jnp.bfloat16
    )
    grad_act = jnp.einsum("slcd,lfd->slcf", scaled, weight_out, preferred_element_type=jnp.float32)
    grad_pre = (grad_act * derivative).astype(jnp.bfloat16)
    grad_w_out = jnp.einsum("slcf,slcd->lfd", activated, scaled, preferred_element_type=jnp.float32)
    return (grad_pre, scores, grad_w_out.astype(jnp.bfloat16))


def on_device(activations, out_grad, expert_ids, gate_weights, weight_in, weight_out):
    model_width = activations.shape[1]
    local_experts = weight_in.shape[0]
    tensor_size = lax.axis_size("tensor")
    expert_size = lax.axis_size("expert")
    group_in, group_grad = (
        lax.all_gather(activations, "tensor", axis=0, tiled=True),
        lax.all_gather(out_grad, "tensor", axis=0, tiled=True),
    )
    table = pick_table(
        slot_places(expert_ids, tensor_size, CAP, EXPERTS), EXPERTS * tensor_size * CAP
    )
    packed_in, packed_grad, packed_gate = pack_slots(table, group_in, group_grad, gate_weights)
    buffer_shape = (expert_size, local_experts, tensor_size * CAP, model_width)
    routed = (
        lax.all_to_all(
            packed_in.reshape(buffer_shape), "expert", split_axis=0, concat_axis=0, tiled=True
        ),
        lax.all_to_all(
            packed_grad.reshape(buffer_shape), "expert", split_axis=0, concat_axis=0, tiled=True
        ),
        lax.all_to_all(
            packed_gate.reshape(buffer_shape[:3]), "expert", split_axis=0, concat_axis=0, tiled=True
        ),
    )
    grad_pre, scores, grad_w_out = expert_math(
        routed[0], routed[1], routed[2], weight_in, weight_out
    )
    partial_value = jnp.einsum(
        "slcf,ldf->slcd", grad_pre, weight_in, preferred_element_type=jnp.float32
    ).astype(jnp.bfloat16)
    back_rows = lax.all_to_all(partial_value, "expert", split_axis=0, concat_axis=0, tiled=True)
    back_scores = lax.all_to_all(scores, "expert", split_axis=0, concat_axis=0, tiled=True)
    spread = jnp.sum(table, axis=1).astype(jnp.bfloat16)
    row_part = jnp.dot(
        spread, back_rows.reshape(-1, model_width), preferred_element_type=jnp.float32
    )
    score_part = jnp.sum(table * back_scores.reshape(-1)[None, None, :], axis=2)
    grad_in = lax.psum_scatter(
        row_part.astype(jnp.bfloat16), "tensor", scatter_dimension=0, tiled=True
    )
    grad_gates = lax.psum_scatter(score_part, "tensor", scatter_dimension=0, tiled=True)
    return (grad_in, grad_gates, grad_w_out)


def solution(mesh):
    return jax.shard_map(
        on_device,
        mesh=mesh,
        in_specs=(
            P(("expert", "tensor"), None),
            P(("expert", "tensor"), None),
            P("expert", None),
            P("expert", None),
            P("expert", None, "tensor"),
            P("expert", "tensor", None),
        ),
        out_specs=(
            P(("expert", "tensor"), None),
            P(("expert", "tensor"), None),
            P("expert", "tensor", None),
        ),
        check_vma=False,
    )
```

profile of v0, /device:TPU:1, one launch (start us, length us, event | category | flops | bytes accessed | tf_op | source)
XLA Modules:
  0.0 796.9 jit_solution(2176635907903466142)
XLA Ops:
  7.2 0.0 copy-start
  7.2 0.0 all-gather.5.cloned.1.call-start
  7.2 0.7 all-gather.5.cloned.1.call-update
  7.9 1.7 fusion.55
  9.6 1.2 reduce_window_sum.13
  10.9 0.9 fusion.54
  11.8 0.7 fusion.58
  12.5 52.0 %all-gather.5.cloned.1.call-done = bf16[512,4096]{1,0:T(8,128)(2,1)} async-done(((bf16[128,4096]{1,0:T(8,128)(2,1)}), bf16[512,4096]{1,0:T(8,128)(2,1)}) %all-gather.5.cloned.1.call-update) | async-done | bytes 4194320 | tf_op jit(solution)/shard_map/all_gather | solution.py:67
  64.5 7.8 convolution_convert_fusion
  72.2 9.8 %reshape.368 = bf16[64,1,12,4096]{3,2,0,1:T(8,128)(2,1)} reshape(bf16[768,4096]{1,0:T(8,128)(2,1)} %convolution_convert_fusion) | data formatting | bytes 12582912 | tf_op jit(solution)/shard_map/reshape | solution.py:77
  82.0 10.9 %all-to-all-start.2 = ((bf16[64,1,12,4096]{3,2,1,0:T(8,128)(2,1)}), bf16[64,1,12,4096]{3,2,1,0:T(8,128)(2,1)}, u32[]{:S(2)}, u32[]{:S(2)}) async-start(bf16[64,1,12,4096]{3,2,1,0:T(8,128)(2,1)} %bitcast.107), calls=%async_computation.2 | async-start | bytes 16777216 | tf_op jit(solution)/shard_map/all_to_all | solution.py:76
  92.9 0.0 all-gather.3.cloned.1.call-start
  93.0 0.7 all-gather.3.cloned.1.call-update
  93.7 52.7 %all-gather.3.cloned.1.call-done = bf16[512,4096]{1,0:T(8,128)(2,1)} async-done(((bf16[128,4096]{1,0:T(8,128)(2,1)}), bf16[512,4096]{1,0:T(8,128)(2,1)}) %all-gather.3.cloned.1.call-update) | async-done | bytes 4194320 | tf_op jit(solution)/shard_map/all_gather | solution.py:68
  146.4 7.8 convolution_convert_fusion.1
  154.2 9.8 %reshape.365 = bf16[64,1,12,4096]{3,2,0,1:T(8,128)(2,1)} reshape(bf16[768,4096]{1,0:T(8,128)(2,1)} %convolution_convert_fusion.1) | data formatting | bytes 12582912 | tf_op jit(solution)/shard_map/reshape | solution.py:80
  163.9 114.8 %all-to-all-done.2 = bf16[64,1,12,4096]{3,2,1,0:T(8,128)(2,1)} async-done(((bf16[64,1,12,4096]{3,2,1,0:T(8,128)(2,1)}), bf16[64,1,12,4096]{3,2,1,0:T(8,128)(2,1)}, u32[]{:S(2)}, u32[]{:S(2)}) %all-to-all-start.2) | async-done | bytes 6291488 | tf_op jit(solution)/shard_map/all_to_all | solution.py:76
  278.7 6.7 all-to-all-start.1
  285.4 0.0 copy-done
  285.4 9.4 %fusion.24 = f32[64,1,12,384]{3,0,2,1:T(8,128)} fusion(bf16[1,4096,384]{2,1,0:T(8,128)(2,1)S(1)} %copy-done, bf16[64,1,12,4096]{3,2,1,0:T(8,128)(2,1)} %all-to-all-done.2), kind=kOutput, calls=%fused_computation.31 | convolution fusion | flops 2415919104 | bytes 10616832 | tf_op jit(solution)/shard_map/slcd,ldf->slcf/dot_general | solution.py:44
  294.8 0.0 copy-start.1
  294.8 176.2 %all-to-all-done.1 = bf16[64,1,12,4096]{3,2,1,0:T(8,128)(2,1)} async-done(((bf16[64,1,12,4096]{3,2,1,0:T(8,128)(2,1)}), bf16[64,1,12,4096]{3,2,1,0:T(8,128)(2,1)}, u32[]{:S(2)}, u32[]{:S(2)}) %all-to-all-start.1) | async-done | bytes 6291488 | tf_op jit(solution)/shard_map/all_to_all | solution.py:79
  471.0 13.1 %fusion.1 = f32[64,12]{0,1:T(8,128)S(1)} fusion(bf16[1,384,4096]{2,1,0:T(8,128)(2,1)} %param.11, bf16[64,1,12,4096]{3,2,1,0:T(8,128)(2,1)} %all-to-all-done.1, f32[64,1,12,384]{3,0,2,1:T(8,128)} %fusion.24), kind=kOutput, calls=%fused_computation.3 | convolution fusion | flops 2426830080 | bytes 10619904 | tf_op jit(solution)/shard_map/slcf,lfd->slcd/dot_general | solution.py:48
  484.1 0.7 copy.30
  484.8 5.9 all-to-all-start.4
  490.8 0.0 copy-done.1
  490.8 9.2 %all-to-all-done.4 = f32[64,1,12]{2,1,0:T(1,128)S(1)} async-done(((f32[64,1,12]{2,1,0:T(1,128)}), f32[64,1,12]{2,1,0:T(1,128)S(1)}, u32[]{:S(2)}, u32[]{:S(2)}) %all-to-all-start.4) | async-done | bytes 3104 | tf_op jit(solution)/shard_map/all_to_all | solution.py:93
  500.0 0.5 broadcast.227
  500.5 0.7 reduce.6
  501.2 0.1 mul.116
  501.3 0.5 select_reduce_fusion
  501.8 0.1 convert_element_type.142
  502.0 13.3 %all_to_all.25 = bf16[64,1,12]{2,1,0:T(2,128)(2,1)S(1)} all-to-all(bf16[64,1,12]{2,1,0:T(2,128)(2,1)S(1)} %convert_element_type.142), channel_id=1, replica_groups=mesh['expert'=64,'tensor'=4] {'expert'}, dimensions={0} | all-to-all | bytes 3072 | tf_op jit(solution)/shard_map/all_to_all | solution.py:82
  515.3 0.1 copy.24
  515.4 9.5 %fusion.39 = bf16[64,12,384]{2,0,1:T(8,128)(2,1)S(1)} fusion(bf16[1,384,4096]{2,1,0:T(8,128)(2,1)} %param.11, f32[64,12]{0,1:T(8,128)S(1)} %copy.24, bf16[64,1,12,4096]{3,2,1,0:T(8,128)(2,1)} %all-to-all-done.1, f32[64,1,12,384]{3,0,2,1:T(8,128)} %fusion.24), kind=kOutput, calls=%fused_computation.34 | convolution fusion | flops 2428305408 | bytes 11209728 | tf_op jit(solution)/shard_map/slcd,lfd->slcf/dot_general | solution.py:55
  524.8 3.7 fusion.6
  528.5 6.8 copy.29
  535.3 6.0 all-to-all-start.3
  541.3 0.0 reduce-scatter.7.cloned.1.call-start
  541.4 0.8 copy.31
  542.2 0.0 reduce-scatter.7.cloned.1.call-update
  542.2 0.0 reduce-scatter.5.cloned.1.call-start
  542.3 184.8 %all-to-all-done.3 = bf16[64,1,12,4096]{3,2,1,0:T(8,128)(2,1)} async-done(((bf16[64,1,12,4096]{3,2,1,0:T(8,128)(2,1)}), bf16[64,1,12,4096]{3,2,1,0:T(8,128)(2,1)}, u32[]{:S(2)}, u32[]{:S(2)}) %all-to-all-start.3) | async-done | bytes 6291488 | tf_op jit(solution)/shard_map/all_to_all | solution.py:92
  727.1 9.9 %reshape.372 = bf16[768,4096]{1,0:T(8,128)(2,1)} reshape(bf16[64,1,12,4096]{3,2,1,0:T(8,128)(2,1)} %all-to-all-done.3) | data formatting | bytes 12582912 | tf_op jit(solution)/shard_map/reshape | solution.py:96
  737.1 7.8 convolution_convert_fusion.3
  744.9 0.0 reduce-scatter.5.cloned.1.call-update
  745.0 14.0 %fusion.10 = bf16[1,384,4096]{2,1,0:T(8,128)(2,1)} fusion(f32[64,12]{0,1:T(8,128)S(1)} %copy.24, bf16[64,1,12,4096]{3,2,1,0:T(8,128)(2,1)} %all-to-all-done.1, f32[64,1,12,384]{3,0,2,1:T(8,128)} %fusion.24), kind=kOutput, calls=%fused_computation.15 | convolution fusion | flops 2428403712 | bytes 10619904 | tf_op jit(solution)/shard_map/slcf,slcd->lfd/dot_general | solution.py:57
  758.9 0.0 reduce-scatter.7.cloned.1.call-done
  758.9 1.4 copy.32
  760.3 29.8 %reduce-scatter.5.cloned.1.call-done = bf16[128,4096]{1,0:T(8,128)(2,1)} async-done(((bf16[512,4096]{1,0:T(8,128)(2,1)}), bf16[128,4096]{1,0:T(8,128)(2,1)}) %reduce-scatter.5.cloned.1.call-update) | async-done | bytes 1048592 | tf_op jit(solution)/shard_map/reduce_scatter | solution.py:99
  (2 shorter events, 0.0 us)
Async XLA Ops:
  7.2 278.3 %copy-start = (bf16[1,4096,384]{2,1,0:T(8,128)(2,1)S(1)}, bf16[1,4096,384]{2,1,0:T(8,128)(2,1)}, u32[]{:S(2)}) copy-start(bf16[1,4096,384]{2,1,0:T(8,128)(2,1)} %param.10) | copy-start | bytes 9437188
  7.2 57.3 %all-gather.5.cloned.1.call-start = ((), (), s32[]{:S(2)}) async-start(), calls=%async_computation.8 | async-start | bytes 5242880 | tf_op jit(solution)/shard_map/all_gather | solution.py:67
  82.0 196.7 %all-to-all-start.2 = ((bf16[64,1,12,4096]{3,2,1,0:T(8,128)(2,1)}), bf16[64,1,12,4096]{3,2,1,0:T(8,128)(2,1)}, u32[]{:S(2)}, u32[]{:S(2)}) async-start(bf16[64,1,12,4096]{3,2,1,0:T(8,128)(2,1)} %bitcast.107), calls=%async_computation.2 | async-start | bytes 16777216 | tf_op jit(solution)/shard_map/all_to_all | solution.py:76
  92.9 53.5 %all-gather.3.cloned.1.call-start = ((), (), s32[]{:S(2)}) async-start(), calls=%async_computation.7 | async-start | bytes 5242880 | tf_op jit(solution)/shard_map/all_gather | solution.py:68
  278.7 192.3 %all-to-all-start.1 = ((bf16[64,1,12,4096]{3,2,1,0:T(8,128)(2,1)}), bf16[64,1,12,4096]{3,2,1,0:T(8,128)(2,1)}, u32[]{:S(2)}, u32[]{:S(2)}) async-start(bf16[64,1,12,4096]{3,2,1,0:T(8,128)(2,1)} %bitcast.108), calls=%async_computation.1 | async-start | bytes 16777216 | tf_op jit(solution)/shard_map/all_to_all | solution.py:79
  294.8 195.9 %copy-start.1 = (bf16[512,1]{0,1:T(2,128)(2,1)S(1)}, bf16[512,1]{0,1:T(2,128)(2,1)}, u32[]{:S(2)}) copy-start(bf16[512,1]{0,1:T(2,128)(2,1)} %param.9) | copy-start | bytes 3076
  484.8 15.1 %all-to-all-start.4 = ((f32[64,1,12]{2,1,0:T(1,128)}), f32[64,1,12]{2,1,0:T(1,128)S(1)}, u32[]{:S(2)}, u32[]{:S(2)}) async-start(f32[64,1,12]{2,1,0:T(1,128)} %copy.30), calls=%async_computation.5 | async-start | bytes 65536 | tf_op jit(solution)/shard_map/all_to_all | solution.py:93
  535.3 191.8 %all-to-all-start.3 = ((bf16[64,1,12,4096]{3,2,1,0:T(8,128)(2,1)}), bf16[64,1,12,4096]{3,2,1,0:T(8,128)(2,1)}, u32[]{:S(2)}, u32[]{:S(2)}) async-start(bf16[64,1,12,4096]{3,2,1,0:T(8,128)(2,1)} %copy.29), calls=%async_computation.3 | async-start | bytes 16777216 | tf_op jit(solution)/shard_map/all_to_all | solution.py:92
  541.3 217.6 %reduce-scatter.7.cloned.1.call-start = ((), (), s32[]{:S(2)}) async-start(), calls=%async_computation.10 | async-start | bytes 327680
  542.2 247.9 %reduce-scatter.5.cloned.1.call-start = ((), (), s32[]{:S(2)}) async-start(), calls=%async_computation.9 | async-start | bytes 5242880 | tf_op jit(solution)/shard_map/reduce_scatter | solution.py:99
Sparse Core Ops, SparseCore 0:
  9.8 54.5 all-gather.4
  95.6 50.7 all-gather.2
  544.7 21.8 reduce-scatter.6
  745.1 45.0 reduce-scatter.4
where the time goes:
time: 803 us; the launch traced here: 797 us
  waiting for transfers between devices  621 us (77%)
  matrix products  73 us (9%)
  local copies, waits for them, and re-layouts  40.1 us (5%)
  starting transfers between devices  29.7 us (4%)
  between operations  14.1 us (2%)
  blocking collectives  13.3 us (2%)
    all_to_all x1, waiting for transfers between devices, on_device(): lax.all_to_all(partial_value, 'expert', split_axis=0, concat_axis=0, tile...  185 us
    all_to_all x1, waiting for transfers between devices, on_device(): lax.all_to_all(packed_grad.reshape(buffer_shape), 'expert', split_axis=0,...  176 us
    all_to_all x1, waiting for transfers between devices, on_device(): lax.all_to_all(packed_in.reshape(buffer_shape), 'expert', split_axis=0, c...  115 us
    all_gather x1, waiting for transfers between devices, on_device(): lax.all_gather(out_grad, 'tensor', axis=0, tiled=True)  52.7 us
    all_gather x1, waiting for transfers between devices, on_device(): lax.all_gather(activations, 'tensor', axis=0, tiled=True)  52 us
    reduce_scatter x1, waiting for transfers between devices, on_device(): lax.psum_scatter(row_part.astype(jnp.bfloat16), 'tensor', scatter_dimensi...  29.8 us
  transfers between devices with their start and end apart: 8, of which 7 were waited for; matrix products, arithmetic and copies ran while one was open for 8% of the time, Pallas kernels for 0%

commit v1 on v0

v1 whole, which is shorter than its diff:
```python
import jax
import jax.numpy as jnp
from jax import lax
from jax.sharding import PartitionSpec as P

EXPERTS = 64
CAP = 3
ROOT_HALF = 0.7071067811865476
INV_ROOT_TAU = 0.3989422804014327


def own_slots(expert_ids):
    rows = expert_ids.shape[0]
    same = expert_ids[:, None] == expert_ids[None, :]
    before = jnp.arange(rows)[None, :] < jnp.arange(rows)[:, None]
    position = jnp.sum((same & before).astype(jnp.int32), axis=1)
    return expert_ids * CAP + position


def on_device(activations, out_grad, expert_ids, gate_weights, weight_in, weight_out):
    rows, width = activations.shape
    expert_size = lax.axis_size("expert")
    tensor_size = lax.axis_size("tensor")
    first = lax.axis_index("tensor") * rows
    ids = lax.dynamic_slice_in_dim(expert_ids[:, 0], first, rows)
    gates = lax.dynamic_slice_in_dim(gate_weights[:, 0], first, rows).astype(jnp.float32)
    slots = own_slots(ids)
    table = slots[:, None] == jnp.arange(EXPERTS * CAP, dtype=jnp.int32)
    spread = table.astype(jnp.bfloat16)
    scaled = (gates[:, None] * out_grad.astype(jnp.float32)).astype(jnp.bfloat16)

    def dispatch(values):
        packed = jnp.dot(spread.T, values, preferred_element_type=jnp.float32)
        packed = packed.astype(jnp.bfloat16).reshape(expert_size, CAP, width)
        there = lax.all_to_all(packed, "expert", split_axis=0, concat_axis=0, tiled=True)
        there = there.reshape(expert_size * CAP, width)
        return lax.all_gather(there, "tensor", axis=0, tiled=True)

    inputs = dispatch(activations)
    grads = dispatch(scaled)
    w_in, w_out = weight_in[0], weight_out[0]
    pre = jnp.dot(inputs, w_in, preferred_element_type=jnp.float32)
    cdf = 0.5 * (1.0 + lax.erf(pre * ROOT_HALF))
    activated = pre * cdf
    slope = cdf + pre * INV_ROOT_TAU * jnp.exp(-0.5 * pre * pre)
    grad_act = jnp.einsum("rd,fd->rf", grads, w_out, preferred_element_type=jnp.float32)
    activated = activated.astype(jnp.bfloat16)
    scores = jnp.sum(activated.astype(jnp.float32) * grad_act, axis=1)
    grad_pre = (grad_act * slope).astype(jnp.bfloat16)
    grad_w_out = jnp.einsum("rf,rd->fd", activated, grads, preferred_element_type=jnp.float32)
    partial = jnp.einsum("rf,df->rd", grad_pre, w_in, preferred_element_type=jnp.float32)
    partial = partial.astype(jnp.bfloat16)
    mine = lax.psum_scatter(partial, "tensor", scatter_dimension=0, tiled=True)
    back = lax.all_to_all(
        mine.reshape(expert_size, CAP, width), "expert", split_axis=0, concat_axis=0, tiled=True
    )
    my_scores = lax.psum_scatter(scores, "tensor", scatter_dimension=0, tiled=True)
    back_scores = lax.all_to_all(
        my_scores.reshape(expert_size, CAP), "expert", split_axis=0, concat_axis=0, tiled=True
    )
    grad_in = jnp.dot(
        spread, back.reshape(-1, width), preferred_element_type=jnp.float32
    ).astype(jnp.bfloat16)
    grad_gates = jnp.sum(jnp.where(table, back_scores.reshape(1, -1), 0.0), axis=1) / gates
    return (grad_in, grad_gates[:, None], grad_w_out.astype(jnp.bfloat16)[None])


def solution(mesh):
    return jax.shard_map(
        on_device,
        mesh=mesh,
        in_specs=(
            P(("expert", "tensor"), None),
            P(("expert", "tensor"), None),
            P("expert", None),
            P("expert", None),
            P("expert", None, "tensor"),
            P("expert", "tensor", None),
        ),
        out_specs=(
            P(("expert", "tensor"), None),
            P(("expert", "tensor"), None),
            P("expert", "tensor", None),
        ),
        check_vma=False,
    )
```

time: 803 us -> 382 us (0.48)
  waiting for transfers between devices: 621 us -> 147 us
  blocking collectives: 13.3 us -> 129 us
  matrix products: 73 us -> 35.4 us
  local copies, waits for them, and re-layouts: 40.1 us -> 29.2 us
    all_to_all x4 -> x2, waiting for transfers between devices: 485 us -> 41.7 us  [the longest x1 41.7 us: on_device(): lax.all_to_all(mine.reshape(expert_size, CAP, width), 'expert', split_axi...]
    all_to_all x1 -> x2, blocking collectives: 13.3 us -> 122 us  [dispatch(): lax.all_to_all(packed, 'expert', split_axis=0, concat_axis=0, tiled=True)]
    all_gather x2, waiting for transfers between devices: 105 us -> 60.4 us  [dispatch(): return lax.all_gather(there, 'tensor', axis=0, tiled=True)]
    dot_general x8 -> x7, matrix products: 73 us -> 35.4 us  [the longest x1 7.44 us: on_device(): jnp.einsum('rf,rd->fd', activated, grads, preferred_element_type=jnp.floa...]
    reduce_scatter x1, waiting for transfers between devices: 29.8 us -> 44.8 us  [on_device(): mine = lax.psum_scatter(partial, 'tensor', scatter_dimension=0, tiled=True)]
    all_to_all x4 -> x2, starting transfers between devices: 29.6 us -> 23.8 us  [the longest x1 13 us: on_device(): lax.all_to_all(my_scores.reshape(expert_size, CAP), 'expert', split_axis=...]
    reshape x3 -> x6, local copies, waits for them, and re-layouts: 29.5 us -> 25.1 us  [the longest x2 8.55 us: dispatch(): there = there.reshape(expert_size * CAP, width)]
  transfers between devices with their start and end apart: 8 -> 5, of which waited for: 7 -> 3; matrix products, arithmetic and copies ran while one was open for 8% -> 8% of each run, Pallas kernels for 0% -> 0%
where the time goes in v1:
time: 382 us; the launch traced here: 381 us
  waiting for transfers between devices  147 us (38%)
  blocking collectives  129 us (34%)
  matrix products  35.4 us (9%)
  local copies, waits for them, and re-layouts  29.2 us (8%)
  starting transfers between devices  24 us (6%)
  between operations  14.5 us (4%)
    all_to_all x2, blocking collectives, dispatch(): lax.all_to_all(packed, 'expert', split_axis=0, concat_axis=0, tiled=True)  122 us
    all_gather x2, waiting for transfers between devices, dispatch(): return lax.all_gather(there, 'tensor', axis=0, tiled=True)  60.4 us
    reduce_scatter x1, waiting for transfers between devices, on_device(): mine = lax.psum_scatter(partial, 'tensor', scatter_dimension=0, tiled=True)  44.8 us
    all_to_all x1, waiting for transfers between devices, on_device(): lax.all_to_all(mine.reshape(expert_size, CAP, width), 'expert', split_axi...  41.7 us
    all_to_all x1, starting transfers between devices, on_device(): lax.all_to_all(my_scores.reshape(expert_size, CAP), 'expert', split_axis=...  13 us
    all_to_all x1, starting transfers between devices, on_device(): lax.all_to_all(mine.reshape(expert_size, CAP, width), 'expert', split_axi...  10.8 us
    reshape x2, local copies, waits for them, and re-layouts, dispatch(): there = there.reshape(expert_size * CAP, width)  8.55 us
    reshape x2, local copies, waits for them, and re-layouts, dispatch(): packed = packed.astype(jnp.bfloat16).reshape(expert_size, CAP, width)  8.14 us
  transfers between devices with their start and end apart: 5, of which 3 were waited for; matrix products, arithmetic and copies ran while one was open for 8% of the time, Pallas kernels for 0%

profile of v1, /device:TPU:1, one launch (start us, length us, event | category | flops | bytes accessed | tf_op | source)
XLA Modules:
  0.0 380.8 jit_solution(5960654569417645199)
XLA Ops:
  7.2 0.0 copy-start
  7.2 0.0 all-gather.5.cloned.1.call-start
  7.2 0.8 fusion.20
  8.0 0.2 convert_reduce_fusion
  8.2 0.7 fusion.19
  8.9 2.9 convolution_convert_fusion.2
  11.8 4.1 %reshape.40 = bf16[64,3,4096]{2,1,0:T(4,128)(2,1)} reshape(bf16[192,4096]{1,0:T(8,128)(2,1)} %convolution_convert_fusion.2) | data formatting | bytes 3145728 | tf_op jit(solution)/shard_map/reshape | solution.py:34
  15.9 64.5 %all_to_all.24 = bf16[64,3,4096]{2,1,0:T(4,128)(2,1)} all-to-all(bf16[64,3,4096]{2,1,0:T(4,128)(2,1)} %reshape.40), channel_id=1, replica_groups=mesh['expert'=64,'tensor'=4] {'expert'}, dimensions={0} | all-to-all | bytes 3145728 | tf_op jit(solution)/shard_map/all_to_all | solution.py:35
  80.4 4.3 %reshape.41 = bf16[192,4096]{1,0:T(8,128)(2,1)} reshape(bf16[64,3,4096]{2,1,0:T(4,128)(2,1)} %all_to_all.24) | data formatting | bytes 3145728 | tf_op jit(solution)/shard_map/reshape | solution.py:36
  84.7 0.0 copy-start.1
  84.7 0.0 all-gather.5.cloned.1.call-update
  84.7 0.0 all-gather.3.cloned.1.call-start
  84.8 0.6 copy-done.1
  85.4 3.0 convolution_convert_fusion.3
  88.4 4.1 %reshape.38 = bf16[64,3,4096]{2,1,0:T(4,128)(2,1)} reshape(bf16[192,4096]{1,0:T(8,128)(2,1)} %convolution_convert_fusion.3) | data formatting | bytes 3145728 | tf_op jit(solution)/shard_map/reshape | solution.py:34
  92.5 57.2 %all_to_all.25 = bf16[64,3,4096]{2,1,0:T(4,128)(2,1)} all-to-all(bf16[64,3,4096]{2,1,0:T(4,128)(2,1)} %reshape.38), channel_id=1, replica_groups=mesh['expert'=64,'tensor'=4] {'expert'}, dimensions={0} | all-to-all | bytes 3145728 | tf_op jit(solution)/shard_map/all_to_all | solution.py:35
  149.6 4.3 %reshape.39 = bf16[192,4096]{1,0:T(8,128)(2,1)} reshape(bf16[64,3,4096]{2,1,0:T(4,128)(2,1)} %all_to_all.25) | data formatting | bytes 3145728 | tf_op jit(solution)/shard_map/reshape | solution.py:36
  153.9 0.0 all-gather.3.cloned.1.call-update
  153.9 0.0 reduce-scatter.2.cloned.1.call-start
  154.0 0.0 all-gather.5.cloned.1.call-done
  154.0 0.0 copy-done
  154.0 6.5 %fusion.2 = f32[768,384]{0,1:T(8,128)} fusion(bf16[768,4096]{1,0:T(8,128)(2,1)} %all-gather.5.cloned.1.call-done, bf16[1,4096,384]{2,1,0:T(8,128)(2,1)S(1)} %copy-done), kind=kOutput, calls=%fused_computation.7 | convolution fusion | flops 2415919104 | bytes 10616832 | tf_op jit(solution)/shard_map/dot_general | solution.py:42
  160.5 60.4 %all-gather.3.cloned.1.call-done = bf16[768,4096]{1,0:T(8,128)(2,1)} async-done(((bf16[192,4096]{1,0:T(8,128)(2,1)}), bf16[768,4096]{1,0:T(8,128)(2,1)}) %all-gather.3.cloned.1.call-update) | async-done | bytes 6291472 | tf_op jit(solution)/shard_map/all_gather | solution.py:37
  220.9 0.0 copy-start.3
  220.9 6.8 %multiply_reduce_fusion = (f32[768]{0:T(1024)S(1)}, f32[768,384]{0,1:T(8,128)S(1)}) fusion(f32[768,384]{0,1:T(8,128)} %fusion.2, bf16[768,4096]{1,0:T(8,128)(2,1)} %all-gather.3.cloned.1.call-done, bf16[1,384,4096]{2,1,0:T(8,128)(2,1)} %param.11), kind=kOutput, calls=%fused_computation.18 | convolution fusion | flops 2418277632 | bytes 11799552 | tf_op jit(solution)/shard_map/rd,fd->rf/dot_general | solution.py:46
  227.6 0.0 copy-done.3
  227.6 5.9 %convolution_convert_fusion = bf16[768,4096]{1,0:T(8,128)(2,1)} fusion(bf16[1,4096,384]{2,1,0:T(8,128)(2,1)S(1)} %copy-done, f32[768,384]{0,1:T(8,128)S(1)} %get-tuple-element.4, f32[768,384]{0,1:T(8,128)S(1)} %copy-done.3), kind=kOutput, calls=%fused_computation | convolution fusion | flops 2422013952 | bytes 11796480 | tf_op jit(solution)/shard_map/rf,df->rd/dot_general | solution.py:51
  233.5 0.0 copy-start.2
  233.5 0.0 reduce-scatter.2.cloned.1.call-update
  233.6 0.6 copy-done.2
  234.2 0.6 dynamic-slice.2
  235.5 6.9 %all-reduce = f32[768]{0:T(1024)S(1)} all-reduce(f32[768]{0:T(1024)S(1)} %get-tuple-element.3), channel_id=3, replica_groups=mesh['expert'=64,'tensor'=4] {'tensor'}, use_global_device_ids=true, to_apply=%region_3.0.clone | all-reduce | flops 768 | bytes 6144
  242.4 0.1 dynamic-slice.3
  242.5 0.8 all_to_all.18
  243.2 13.0 %all-to-all-start.3 = ((f32[64,1,3]{2,1,0:T(1,128)}), f32[64,1,3]{2,1,0:T(1,128)S(1)}, u32[]{:S(2)}, u32[]{:S(2)}) async-start(f32[64,1,3]{2,1,0:T(1,128)} %bitcast.6), calls=%async_computation.4 | async-start | bytes 65536 | tf_op jit(solution)/shard_map/all_to_all | solution.py:58
  256.2 44.8 %reduce-scatter.2.cloned.1.call-done = bf16[192,4096]{1,0:T(8,128)(2,1)} async-done(((bf16[768,4096]{1,0:T(8,128)(2,1)}), bf16[192,4096]{1,0:T(8,128)(2,1)}) %reduce-scatter.2.cloned.1.call-update) | async-done | bytes 1572880 | tf_op jit(solution)/shard_map/reduce_scatter | solution.py:53
  301.0 4.1 %reshape.42 = bf16[64,3,4096]{2,1,0:T(4,128)(2,1)} reshape(bf16[192,4096]{1,0:T(8,128)(2,1)} %reduce-scatter.2.cloned.1.call-done) | data formatting | bytes 3145728 | tf_op jit(solution)/shard_map/reshape | solution.py:55
  305.1 0.0 all-to-all-done.3
  305.1 10.8 %all-to-all-start.2 = ((bf16[64,3,4096]{2,1,0:T(4,128)(2,1)}), bf16[64,3,4096]{2,1,0:T(4,128)(2,1)}, u32[]{:S(2)}, u32[]{:S(2)}) async-start(bf16[64,3,4096]{2,1,0:T(4,128)(2,1)} %reshape.42), calls=%async_computation.3 | async-start | bytes 4194304 | tf_op jit(solution)/shard_map/all_to_all | solution.py:54
  315.9 7.4 %fusion = bf16[1,384,4096]{2,1,0:T(8,128)(2,1)} fusion(bf16[768,4096]{1,0:T(8,128)(2,1)} %all-gather.3.cloned.1.call-done, f32[768,384]{0,1:T(8,128)} %fusion.2), kind=kOutput, calls=%fused_computation.2 | convolution fusion | flops 2418966528 | bytes 10616832 | tf_op jit(solution)/shard_map/rf,rd->fd/dot_general | solution.py:50
  323.4 0.5 broadcast.4
  323.9 0.7 reduce.3
  324.6 0.1 broadcast_in_dim.16
  324.8 0.1 select_reduce_fusion
  324.9 0.5 bitcast_divide_fusion
  325.4 41.7 %all-to-all-done.2 = bf16[64,3,4096]{2,1,0:T(4,128)(2,1)} async-done(((bf16[64,3,4096]{2,1,0:T(4,128)(2,1)}), bf16[64,3,4096]{2,1,0:T(4,128)(2,1)}, u32[]{:S(2)}, u32[]{:S(2)}) %all-to-all-start.2) | async-done | bytes 1572896 | tf_op jit(solution)/shard_map/all_to_all | solution.py:54
  367.1 4.3 %reshape.43 = bf16[192,4096]{1,0:T(8,128)(2,1)} reshape(bf16[64,3,4096]{2,1,0:T(4,128)(2,1)} %all-to-all-done.2) | data formatting | bytes 3145728 | tf_op jit(solution)/shard_map/reshape | solution.py:62
  371.4 2.9 convolution_convert_fusion.4
  (1 shorter events, 0.0 us)
Async XLA Ops:
  7.2 146.8 %copy-start = (bf16[1,4096,384]{2,1,0:T(8,128)(2,1)S(1)}, bf16[1,4096,384]{2,1,0:T(8,128)(2,1)}, u32[]{:S(2)}) copy-start(bf16[1,4096,384]{2,1,0:T(8,128)(2,1)} %param.10) | copy-start | bytes 9437188
  7.2 146.8 %all-gather.5.cloned.1.call-start = ((), (), s32[]{:S(2)}) async-start(), calls=%async_computation.6 | async-start | bytes 7864320 | tf_op jit(solution)/shard_map/all_gather | solution.py:37
  84.7 0.7 copy-start.1
  84.7 136.1 %all-gather.3.cloned.1.call-start = ((), (), s32[]{:S(2)}) async-start(), calls=%async_computation.5 | async-start | bytes 7864320 | tf_op jit(solution)/shard_map/all_gather | solution.py:37
  153.9 147.1 %reduce-scatter.2.cloned.1.call-start = ((), (), s32[]{:S(2)}) async-start(), calls=%async_computation.7 | async-start | bytes 7864320 | tf_op jit(solution)/shard_map/reduce_scatter | solution.py:53
  220.9 6.8 %copy-start.3 = (f32[768,384]{0,1:T(8,128)S(1)}, f32[768,384]{0,1:T(8,128)}, u32[]{:S(2)}) copy-start(f32[768,384]{0,1:T(8,128)} %fusion.2) | copy-start | bytes 3538948
  233.5 0.7 copy-start.2
  243.2 61.9 %all-to-all-start.3 = ((f32[64,1,3]{2,1,0:T(1,128)}), f32[64,1,3]{2,1,0:T(1,128)S(1)}, u32[]{:S(2)}, u32[]{:S(2)}) async-start(f32[64,1,3]{2,1,0:T(1,128)} %bitcast.6), calls=%async_computation.4 | async-start | bytes 65536 | tf_op jit(solution)/shard_map/all_to_all | solution.py:58
  305.1 62.0 %all-to-all-start.2 = ((bf16[64,3,4096]{2,1,0:T(4,128)(2,1)}), bf16[64,3,4096]{2,1,0:T(4,128)(2,1)}, u32[]{:S(2)}, u32[]{:S(2)}) async-start(bf16[64,3,4096]{2,1,0:T(4,128)(2,1)} %reshape.42), calls=%async_computation.3 | async-start | bytes 4194304 | tf_op jit(solution)/shard_map/all_to_all | solution.py:54
Sparse Core Ops, SparseCore 0:
  84.8 64.6 all-gather.4
  154.1 66.7 all-gather.2
  233.7 67.2 reduce-scatter.1
